TPU v7x, 256 devices: a whole 4x4x8 slice. The times are simulated.
256 devices in a mesh: seq: 32 (over z, y), exp: 8 (over x, core).
Axes of the slice: x: 4, y: 4, z: 8, core: 2. Of those that a mesh axis runs over, the one named last changes fastest.
Arguments:
- residual: bfloat16 [4096, 6144], P('exp', 'seq'), may hold values from -8 to 8
- query: bfloat16 [4096, 8192], P('seq', 'exp'), may hold values from -6 to 6
- key_in: bfloat16 [4096, 8192], P('seq', 'exp'), may hold values from -6 to 6
- value_in: bfloat16 [4096, 8192], P('seq', 'exp'), may hold values from -0.75 to 0.75
- gate_in: bfloat16 [4096, 8192], P('seq', 'exp'), may hold values from -6 to 6
- log_decay: float32 [4096, 64], P('seq', 'exp'), may hold values from -2 to 0
- state_in: float32 [64, 128, 128], P('exp'), may hold values from -12 to 12
- attn_gain: float32 [8192], P('exp'), may hold values from 0.1 to 1.9
- w_out: bfloat16 [8192, 6144], P('exp', 'seq'), may hold values from -0.0625 to 0.0625
- moe_gain: float32 [6144], P('seq'), may hold values from 0.1 to 1.9
- router: float32 [6144, 32], P('seq'), may hold values from -0.078125 to 0.078125
- w_gate: bfloat16 [8, 9216, 6144], P('exp', 'seq'), may hold values from -0.078125 to 0.078125
- w_up: bfloat16 [8, 9216, 6144], P('exp', 'seq'), may hold values from -0.078125 to 0.078125
- w_down: bfloat16 [8, 9216, 6144], P('exp', None, 'seq'), may hold values from -0.125 to 0.125
- expert_ids: int32 [4096, 2], P('exp'), may hold values from 0 to 31, all different within a row; in each aligned block of 512 rows (0 to 511, 512 to 1023, ...) at most 40 rows name the same one
- keep_counts: int32 [32], replicated, may hold values from 64 to 319
Outputs:
- layer_out: bfloat16 [4096, 6144], P('exp', 'seq')
- final_state: float32 [64, 128, 128], P('exp', 'seq')
Inputs may be any that keep to these rules, and one draw needn't show every extreme that they name: `expert_ids`: each row names 2 different experts. Among the rows of one device no expert is named more than 40 times, a bound that some block reaches.
All inputs are finite; a program needn't handle non-finite values.
Results may differ from a plain program's by a relative error of at most 0.014.
Values may be sent and summed in bfloat16 or wider, within the bound.
A program may use at most 128 MiB of HBM per device.

v0:
```python
import jax
import jax.numpy as jnp
from jax import lax
from jax.sharding import PartitionSpec as P

D = 6144
epsilon = 1e-05
highest = lax.Precision.HIGHEST


def entering(x, axis, join, neutral):
    place = lax.axis_index(axis)
    gathered = jax.tree.map(
        lambda a, kind: lax.all_gather(a.astype(kind), axis), x, (jnp.bfloat16, jnp.bfloat16)
    )
    state = jax.tree.map(lambda a, e: jnp.zeros_like(a) + jnp.asarray(e, a.dtype), x, neutral)

    def one(lap, state):
        return join(
            state,
            jax.tree.map(
                lambda a, own: lax.dynamic_index_in_dim(a, lap, 0, False).astype(own.dtype),
                gathered,
                x,
            ),
        )

    return lax.fori_loop(0, place, one, state)


def broadcast(value, axis, source):
    kept = jnp.where(lax.axis_index(axis) == source, value, 0).astype(value.dtype)
    return lax.psum(kept, axis)


def entering_2(part, axis, combine, identity):
    place = lax.axis_index(axis)
    gathered = lax.all_gather(part, axis)
    state = jnp.zeros_like(part) + jnp.asarray(identity, part.dtype)

    def one(lap, state):
        return combine(state, lax.dynamic_index_in_dim(gathered, lap, 0, False))

    return lax.fori_loop(0, place, one, state)


def block_terms(act_query, act_key, val_rows, log_rows):
    running_log = jnp.cumsum(log_rows, axis=0)
    block_log = running_log[-1]
    length = log_rows.shape[0]
    causal_mask = (jnp.arange(length)[:, None] >= jnp.arange(length)[None, :])[None]
    flipped = jnp.transpose(running_log)
    log_gap = flipped[:, :, None] - flipped[:, None, :]
    decay_rows = jnp.where(causal_mask, jnp.exp(jnp.where(causal_mask, log_gap, 0.0)), 0.0)
    scores = jnp.einsum("thd,shd->hts", act_query, act_key, precision=highest)
    local_part = jnp.einsum("hts,shd->thd", scores * decay_rows, val_rows, precision=highest)
    tail_decay = jnp.exp(block_log[None, :] - running_log)
    update = jnp.einsum(
        "shd,she->hde", act_key * tail_decay[:, :, None], val_rows, precision=highest
    )
    return (local_part, running_log, block_log, update)


def from_state(act_query, running_log, state_carry):
    return jnp.einsum(
        "thd,hde->the", act_query * jnp.exp(running_log)[:, :, None], state_carry, precision=highest
    )


def join_states(earlier, later_part):
    return (
        earlier[0] + later_part[0],
        jnp.exp(later_part[0])[:, None, None] * earlier[1] + later_part[1],
    )


def add_counts(earlier, later_counts):
    return earlier + later_counts


def local(
    residual,
    query,
    key_in,
    value_in,
    gate_in,
    log_decay,
    state_in,
    attn_gain,
    w_out,
    moe_gain,
    router,
    w_gate,
    w_up,
    w_down,
    expert_ids,
    keep_counts,
):
    tok_rows, head_width = query.shape
    head_count = log_decay.shape[1]
    head_size = head_width // head_count
    act_query = jax.nn.silu(query.astype(jnp.float32)).reshape(tok_rows, head_count, head_size)
    act_key = jax.nn.silu(key_in.astype(jnp.float32)).reshape(tok_rows, head_count, head_size)
    val_rows = value_in.astype(jnp.float32).reshape(tok_rows, head_count, head_size)
    local_part, running_log, block_log, update = block_terms(
        act_query, act_key, val_rows, log_decay
    )
    segments = lax.axis_size("seq")
    position = lax.axis_index("seq")
    row_share = head_size // segments
    identity_pair = (jnp.zeros_like(block_log), jnp.zeros_like(update))
    before_log, before_state = entering((block_log, update), "seq", join_states, identity_pair)
    incoming = jnp.exp(before_log)[:, None, None] * state_in + before_state
    through = jnp.exp(block_log)[:, None, None] * incoming + update
    last_whole = broadcast(through.astype(jnp.bfloat16), "seq", segments - 1).astype(through.dtype)
    final_rows = lax.dynamic_slice_in_dim(last_whole, position * row_share, row_share, 1)
    outputs = local_part + from_state(act_query, running_log, incoming)
    square_mean = jnp.mean(outputs * outputs, axis=2, keepdims=True)
    normed = outputs * lax.rsqrt(square_mean + epsilon) * attn_gain.reshape(head_count, head_size)
    heads_mixed = (
        normed.reshape(tok_rows, head_width) * jax.nn.sigmoid(gate_in.astype(jnp.float32))
    ).astype(jnp.bfloat16)
    gathered = lax.all_gather(heads_mixed, "seq", axis=0, tiled=True)
    block_rows = residual.shape[0]
    projected = lax.psum_scatter(
        jnp.dot(gathered, w_out, preferred_element_type=jnp.float32).astype(jnp.bfloat16),
        "exp",
        scatter_dimension=0,
        tiled=True,
    ).astype(jnp.float32)
    after_attn = residual.astype(jnp.float32) + projected
    experts_all = router.shape[1]
    logit_part = jnp.dot(after_attn * moe_gain, router, precision=highest)
    choose = (
        expert_ids[:, :, None] == jnp.arange(experts_all, dtype=jnp.int32)[None, None, :]
    ).astype(jnp.float32)
    chosen_part = jnp.einsum("tke,te->tk", choose, logit_part, precision=highest)
    squares, chosen = lax.psum((jnp.sum(after_attn * after_attn, axis=1), chosen_part), "seq")
    inv_rms = lax.rsqrt(squares / D + epsilon)
    chosen = chosen * inv_rms[:, None]
    gate_probs = jnp.stack(
        [jax.nn.sigmoid(chosen[:, 0] - chosen[:, 1]), jax.nn.sigmoid(chosen[:, 1] - chosen[:, 0])],
        axis=1,
    )
    routed_in = (after_attn * inv_rms[:, None] * moe_gain).astype(jnp.bfloat16)
    lanes = lax.axis_size("exp")
    window = w_gate.shape[0] * lanes
    capacity = 5 * block_rows * lanes // (2 * lanes * experts_all)
    top_count = expert_ids.shape[1]
    flat_ids = expert_ids.reshape(block_rows * top_count)
    onehot = (flat_ids[:, None] == jnp.arange(window, dtype=jnp.int32)[None, :]).astype(jnp.int32)
    local_rank = jnp.sum((jnp.cumsum(onehot, axis=0) - onehot) * onehot, axis=1)
    before = entering_2(jnp.sum(onehot, axis=0), "exp", add_counts, jnp.zeros((window,), jnp.int32))
    global_rank = local_rank + jnp.sum(before[None, :] * onehot, axis=1)
    limits = jnp.sum(keep_counts[None, :window] * onehot, axis=1)
    is_kept = (flat_ids < window) & (global_rank < limits)
    slot_hot = ((local_rank[:, None] == jnp.arange(capacity)[None, :]) & is_kept[:, None]).astype(
        jnp.int32
    )
    assign_int = onehot[:, :, None] * slot_hot[:, None, :]
    assign_table = assign_int.astype(jnp.bfloat16)
    token_table = jnp.sum(
        assign_int.reshape(block_rows, top_count, window, capacity), axis=1
    ).astype(jnp.bfloat16)
    sending = jnp.einsum(
        "tec,td->ecd", token_table, routed_in, preferred_element_type=jnp.float32
    ).astype(jnp.bfloat16)
    arrived = lax.all_to_all(sending, "exp", split_axis=0, concat_axis=1, tiled=True)
    contract_dims = (((1,), (1,)), ((), ()))
    portion = lax.all_gather(arrived, "seq", axis=2, tiled=True)
    gate_cols = w_gate[0]
    up_cols = w_up[0]
    gate_add = lax.dot_general(
        portion[0], gate_cols, contract_dims, preferred_element_type=jnp.float32
    )
    up_add = lax.dot_general(portion[0], up_cols, contract_dims, preferred_element_type=jnp.float32)
    hidden = (jax.nn.silu(gate_add) * up_add).astype(jnp.bfloat16)
    down_rows = w_down[0]
    result = jnp.dot(
        lax.all_gather(hidden, "seq", axis=1, tiled=True),
        down_rows,
        preferred_element_type=jnp.float32,
    )
    expert_out = result.astype(jnp.bfloat16)[None]
    returned = lax.all_to_all(expert_out, "exp", split_axis=1, concat_axis=0, tiled=True)
    picked = jnp.einsum(
        "aec,ecd->ad", assign_table, returned, preferred_element_type=jnp.float32
    ).reshape(block_rows, top_count, -1)
    weight = jnp.where(is_kept.reshape(block_rows, top_count), gate_probs, 0.0)
    expert_sum = jnp.sum(picked * weight[:, :, None], axis=1)
    return ((after_attn + expert_sum).astype(jnp.bfloat16), final_rows)


def solution(mesh):
    in_specs = (
        P("exp", "seq"),
        P("seq", "exp"),
        P("seq", "exp"),
        P("seq", "exp"),
        P("seq", "exp"),
        P("seq", "exp"),
        P("exp", None, None),
        P("exp"),
        P("exp", "seq"),
        P("seq"),
        P("seq", None),
        P("exp", "seq", None),
        P("exp", "seq", None),
        P("exp", None, "seq"),
        P("exp", None),
        P(),
    )
    out_specs = (P("exp", "seq"), P("exp", "seq", None))
    return jax.shard_map(local, mesh=mesh, in_specs=in_specs, out_specs=out_specs, check_vma=False)
```

profile of v0, /device:TPU:2, one launch (start us, length us, event | category | flops | bytes accessed | tf_op | source)
XLA Modules:
  0.0 770.6 jit_solution(17127196625241131130)
XLA Ops:
  15.4 2.1 copy.145
  17.5 2.4 fusion.64
  21.5 42.1 %all-gather.2 = bf16[32,1,8]{2,1,0:T(2,128)(2,1)S(1)} all-gather(bf16[1,1,8]{2,1,0:T(2,128)(2,1)S(1)} %convert_bitcast_fusion), channel_id=1, replica_groups=mesh['seq'=32,'exp'=8] {'seq'}, dimensions={0}, use_global_device_ids=true | all-gather | bytes 528 | tf_op jit(solution)/shard_map/all_gather | solution.py:14
  68.7 52.2 %all-gather.14.cloned.1.call-done = bf16[256,128,128]{2,1,0:T(8,128)(2,1)} async-done(((bf16[8,128,128]{2,1,0:T(8,128)(2,1)}), bf16[256,128,128]{2,1,0:T(8,128)(2,1)}) %all-gather.14.cloned.1.call-update) | async-done | bytes 8388624 | tf_op jit(solution)/shard_map/all_gather | solution.py:14
  121.8 2.7 multiply_reduce_fusion.1
  125.6 2.0 copy.125
  129.6 157.0 %all-gather.8.cloned.1.call-done = bf16[4096,1024]{1,0:T(8,128)(2,1)} async-done(((bf16[128,1024]{1,0:T(8,128)(2,1)}), bf16[4096,1024]{1,0:T(8,128)(2,1)}) %all-gather.8.cloned.1.call-update) | async-done | bytes 8388624 | tf_op jit(solution)/shard_map/all_gather | solution.py:123
  286.6 7.5 convolution_convert_fusion
  300.4 8.1 %all-reduce = s32[64]{0:T(128)S(1)} all-reduce(s32[64]{0:T(128)} %dynamic-update-slice), channel_id=3, replica_groups=mesh['seq'=32,'exp'=8] {'exp'}, use_global_device_ids=true, to_apply=%add | all-reduce | flops 64 | bytes 512
  309.9 5.1 reduce-window.6
  329.5 2.2 fusion.42
  331.7 8.9 %fusion.36 = f32[512,2]{1,0:T(8,128)} fusion(f32[512,32]{1,0:T(8,128)S(1)} %fusion.42, s32[512,2]{1,0:T(8,128)} %copy.126), kind=kLoop, calls=%fused_computation.42 | loop fusion | flops 97280 | bytes 73728
  342.7 73.0 %all-reduce.1 = (f32[512]{0:T(512)}, f32[512,2]{0,1:T(2,128)}) all-reduce(f32[512]{0:T(512)S(1)} %multiply_reduce_fusion.2, f32[512,2]{0,1:T(2,128)S(1)} %copy.141), channel_id=1, replica_groups=mesh['seq'=32,'exp'=8] {'seq'}, use_global_device_ids=true, to_apply=%region_15.16 | all-reduce | flops 1536 | bytes 12288 | tf_op jit(solution)/shard_map/psum | solution.py:138
  420.1 11.7 %all_to_all.24 = bf16[8,40,192]{2,1,0:T(8,128)(2,1)} all-to-all(bf16[8,40,192]{2,1,0:T(8,128)(2,1)S(1)} %convolution_convert_fusion.1), channel_id=1, replica_groups=mesh['seq'=32,'exp'=8] {'exp'}, dimensions={0} | all-to-all | bytes 245760 | tf_op jit(solution)/shard_map/all_to_all | solution.py:168
  433.6 79.5 %all-gather.10.cloned.1.call-done = bf16[1,320,6144]{1,2,0:T(8,128)(2,1)} async-done(((bf16[1,320,192]{1,2,0:T(8,128)(2,1)}), bf16[1,320,6144]{1,2,0:T(8,128)(2,1)}) %all-gather.10.cloned.1.call-update) | async-done | bytes 3932176 | tf_op jit(solution)/shard_map/all_gather | solution.py:170
  513.1 4.5 fusion
  518.0 2.7 fusion.16
  521.4 2.3 fusion.45
  523.7 86.0 %all-gather.12.cloned.1.call-done = bf16[320,9216]{0,1:T(8,128)(2,1)} async-done(((bf16[320,288]{0,1:T(8,128)(2,1)}), bf16[320,9216]{0,1:T(8,128)(2,1)}) %all-gather.12.cloned.1.call-update) | async-done | bytes 5898256 | tf_op jit(solution)/shard_map/all_gather | solution.py:180
  609.7 6.8 fusion.24
  618.8 3.2 reduce.4
  623.8 4.8 all-to-all-start.1
  628.6 127.4 %all-reduce.4.cloned.1.call-done = bf16[8,128,128]{2,1,0:T(8,128)(2,1)} async-done(((bf16[8,128,128]{2,1,0:T(8,128)(2,1)}), bf16[8,128,128]{2,1,0:T(8,128)(2,1)}) %all-reduce.4.cloned.1.call-update) | async-done | bytes 262160 | tf_op jit(solution)/shard_map/psum | solution.py:33
  757.4 2.3 reshape.243
  (96 shorter events, 60.7 us)
Async XLA Ops:
  7.2 506.0 %copy-start = (bf16[1,288,6144]{2,1,0:T(8,128)(2,1)S(1)}, bf16[1,288,6144]{2,1,0:T(8,128)(2,1)}, u32[]{:S(2)}) copy-start(bf16[1,288,6144]{2,1,0:T(8,128)(2,1)} %param.31) | copy-start | bytes 10616836
  7.2 113.7 %all-gather.14.cloned.1.call-start = ((), (), s32[]{:S(2)}) async-start(), calls=%async_computation.8 | async-start | bytes 8650752 | tf_op jit(solution)/shard_map/all_gather | solution.py:14
  19.9 266.7 %all-gather.8.cloned.1.call-start = ((), (), s32[]{:S(2)}) async-start(), calls=%async_computation.3 | async-start | bytes 8650752 | tf_op jit(solution)/shard_map/all_gather | solution.py:123
  65.1 2.0 copy-start.1
  121.7 2.8 copy-start.4
  121.8 3.8 copy-start.5
  129.6 164.6 %copy-start.3 = (s32[512,2]{0,1:T(2,128)S(1)}, s32[512,2]{0,1:T(2,128)}, u32[]{:S(2)}) copy-start(s32[512,2]{0,1:T(2,128)} %param.34) | copy-start | bytes 12292
  129.6 167.7 %copy-start.9 = (u32[256]{0:T(256)S(1)}, u32[256]{0:T(256)}, u32[]{:S(2)}) copy-start(u32[256]{0:T(256)} %constant.77) | copy-start | bytes 3076
  129.6 199.9 %reduce-scatter.2.cloned.1.call-start = ((), (), s32[]{:S(2)}) async-start(), calls=%async_computation.4 | async-start | bytes 1769472 | tf_op jit(solution)/shard_map/reduce_scatter | solution.py:125
  294.2 219.0 %all-gather.10.cloned.1.call-start = ((), (), s32[]{:S(2)}) async-start(), calls=%async_computation.5 | async-start | bytes 4866048 | tf_op jit(solution)/shard_map/all_gather | solution.py:170
  417.8 2.3 copy-start.2
  433.5 176.2 %all-gather.12.cloned.1.call-start = ((), (), s32[]{:S(2)}) async-start(), calls=%async_computation.6 | async-start | bytes 7299072 | tf_op jit(solution)/shard_map/all_gather | solution.py:180
  513.1 4.5 copy-start.7
  513.1 4.9 copy-start.8
  518.0 3.4 copy-start.6
  520.7 235.3 %all-reduce.4.cloned.1.call-start = ((), (), s32[]{:S(2)}) async-start(), calls=%async_computation.7 | async-start | bytes 524288 | tf_op jit(solution)/shard_map/psum | solution.py:33
  623.8 133.5 %all-to-all-start.1 = ((bf16[8,2,3840]{2,1,0:T(2,128)(2,1)}), bf16[8,2,3840]{2,1,0:T(2,128)(2,1)}, u32[]{:S(2)}, u32[]{:S(2)}) async-start(bf16[8,2,3840]{2,1,0:T(2,128)(2,1)} %reshape.242), calls=%async_computation.2 | async-start | bytes 245760 | tf_op jit(solution)/shard_map/all_to_all | solution.py:185
Sparse Core Ops, SparseCore 0:
  20.0 100.8 all-gather.13
  129.7 156.8 all-gather.7
  294.3 29.5 reduce-scatter.1
  433.7 79.4 all-gather.9
  520.8 88.8 all-gather.11
  613.0 142.9 all-reduce.3
where the time goes:
time: 774 us; the launch traced here: 771 us
  waiting for transfers between devices  502 us (65%)
  blocking collectives  135 us (17%)
  other arithmetic  40.5 us (5%)
  local copies, waits for them, and re-layouts  38 us (5%)
  matrix products  34.9 us (5%)
  between operations  15 us (2%)
    all_gather x1, waiting for transfers between devices, local(): gathered = lax.all_gather(heads_mixed, 'seq', axis=0, tiled=True)  157 us
    psum x1, waiting for transfers between devices, broadcast(): return lax.psum(kept, axis)  127 us
    all_gather x1, waiting for transfers between devices, local(): lax.all_gather(hidden, 'seq', axis=1, tiled=True)  86 us
    all_gather x1, waiting for transfers between devices, local(): portion = lax.all_gather(arrived, 'seq', axis=2, tiled=True)  79.5 us
    psum x1, blocking collectives, local(): lax.psum((jnp.sum(after_attn * after_attn, axis=1), chosen_part), 'seq')  73 us
    all_gather x1, waiting for transfers between devices, entering(): lax.all_gather(a.astype(kind), axis)  52.2 us
    all_gather x1, blocking collectives, entering(): lax.all_gather(a.astype(kind), axis)  42.1 us
  transfers between devices with their start and end apart: 7, of which 5 were waited for; matrix products, arithmetic and copies ran while one was open for 7% of the time, Pallas kernels for 0%

commit v1 on v0

--- a/solution.py
+++ b/solution.py
@@ -6,6 +6,12 @@
 D = 6144
 epsilon = 1e-05
 highest = lax.Precision.HIGHEST
+
+
+def add_all(block, mesh_axis):
+    parts = lax.all_gather(block, mesh_axis, axis=0, tiled=False)
+    result = parts.sum(axis=0)
+    return result
 
 
 def entering(x, axis, join, neutral):
@@ -30,7 +36,7 @@
 
 def broadcast(value, axis, source):
     kept = jnp.where(lax.axis_index(axis) == source, value, 0).astype(value.dtype)
-    return lax.psum(kept, axis)
+    return add_all(kept, axis)
 
 
 def entering_2(part, axis, combine, identity):

time: 774 us -> 742 us (0.959)
  waiting for transfers between devices: 502 us -> 463 us
    psum x1 -> x0, waiting for transfers between devices: 127 us -> none  [broadcast(): return lax.psum(kept, axis)]
    all_gather x0 -> x1, waiting for transfers between devices: none -> 89.9 us  [add_all(): parts = lax.all_gather(block, mesh_axis, axis=0, tiled=False)]
  transfers between devices with their start and end apart: 7 -> 7, of which waited for: 5 -> 6; matrix products, arithmetic and copies ran while one was open for 7% -> 7% of each run, Pallas kernels for 0% -> 0%
where the time goes in v1:
time: 742 us; the launch traced here: 737 us
  waiting for transfers between devices  463 us (62%)
  blocking collectives  135 us (18%)
  other arithmetic  46.8 us (6%)
  local copies, waits for them, and re-layouts  38 us (5%)
  matrix products  34.9 us (5%)
  between operations  15 us (2%)
    all_gather x1, waiting for transfers between devices, local(): gathered = lax.all_gather(heads_mixed, 'seq', axis=0, tiled=True)  156 us
    all_gather x1, waiting for transfers between devices, add_all(): parts = lax.all_gather(block, mesh_axis, axis=0, tiled=False)  89.9 us
    all_gather x1, waiting for transfers between devices, local(): lax.all_gather(hidden, 'seq', axis=1, tiled=True)  85 us
    all_gather x1, waiting for transfers between devices, local(): portion = lax.all_gather(arrived, 'seq', axis=2, tiled=True)  76.5 us
    psum x1, blocking collectives, local(): lax.psum((jnp.sum(after_attn * after_attn, axis=1), chosen_part), 'seq')  73 us
    all_gather x1, waiting for transfers between devices, entering(): lax.all_gather(a.astype(kind), axis)  52.2 us
    all_gather x1, blocking collectives, entering(): lax.all_gather(a.astype(kind), axis)  42.1 us
  transfers between devices with their start and end apart: 7, of which 6 were waited for; matrix products, arithmetic and copies ran while one was open for 7% of the time, Pallas kernels for 0%

profile of v1, /device:TPU:2, one launch (start us, length us, event | category | flops | bytes accessed | tf_op | source)
XLA Modules:
  0.0 737.4 jit_solution(5302723025053218818)
XLA Ops:
  17.4 2.4 fusion.64
  21.5 42.1 %all-gather.3 = bf16[32,1,8]{2,1,0:T(2,128)(2,1)S(1)} all-gather(bf16[1,1,8]{2,1,0:T(2,128)(2,1)S(1)} %convert_bitcast_fusion), channel_id=1, replica_groups=mesh['seq'=32,'exp'=8] {'seq'}, dimensions={0}, use_global_device_ids=true | all-gather | bytes 528 | tf_op jit(solution)/shard_map/all_gather | solution.py:20
  68.7 52.2 %all-gather.16.cloned.1.call-done = bf16[256,128,128]{2,1,0:T(8,128)(2,1)} async-done(((bf16[8,128,128]{2,1,0:T(8,128)(2,1)}), bf16[256,128,128]{2,1,0:T(8,128)(2,1)}) %all-gather.16.cloned.1.call-update) | async-done | bytes 8388624 | tf_op jit(solution)/shard_map/all_gather | solution.py:20
  121.7 2.7 multiply_reduce_fusion.1
  129.6 155.6 %all-gather.10.cloned.1.call-done = bf16[4096,1024]{1,0:T(8,128)(2,1)} async-done(((bf16[128,1024]{1,0:T(8,128)(2,1)}), bf16[4096,1024]{1,0:T(8,128)(2,1)}) %all-gather.10.cloned.1.call-update) | async-done | bytes 8388624 | tf_op jit(solution)/shard_map/all_gather | solution.py:129
  285.2 7.5 %convolution_convert_fusion = bf16[4096,192]{0,1:T(8,128)(2,1)} fusion(bf16[4096,1024]{1,0:T(8,128)(2,1)} %all-gather.10.cloned.1.call-done, bf16[1024,192]{0,1:T(8,128)(2,1)} %param.28), kind=kOutput, calls=%fused_computation.5 | convolution fusion | flops 1611399168 | bytes 10354688 | tf_op jit(solution)/shard_map/dot_general | solution.py:132
  299.0 8.1 %all-reduce = s32[64]{0:T(128)S(1)} all-reduce(s32[64]{0:T(128)} %dynamic-update-slice), channel_id=3, replica_groups=mesh['seq'=32,'exp'=8] {'exp'}, use_global_device_ids=true, to_apply=%add | all-reduce | flops 64 | bytes 512
  308.5 5.1 reduce-window.6
  328.1 2.2 fusion.42
  330.3 8.9 %fusion.36 = f32[512,2]{1,0:T(8,128)} fusion(f32[512,32]{1,0:T(8,128)S(1)} %fusion.42, s32[512,2]{1,0:T(8,128)} %copy.126), kind=kLoop, calls=%fused_computation.42 | loop fusion | flops 97280 | bytes 73728
  341.4 73.0 %all-reduce.1 = (f32[512]{0:T(512)}, f32[512,2]{0,1:T(2,128)}) all-reduce(f32[512]{0:T(512)S(1)} %multiply_reduce_fusion.2, f32[512,2]{0,1:T(2,128)S(1)} %copy.141), channel_id=1, replica_groups=mesh['seq'=32,'exp'=8] {'seq'}, use_global_device_ids=true, to_apply=%region_15.16 | all-reduce | flops 1536 | bytes 12288 | tf_op jit(solution)/shard_map/psum | solution.py:144
  418.8 11.7 %all_to_all.24 = bf16[8,40,192]{2,1,0:T(8,128)(2,1)} all-to-all(bf16[8,40,192]{2,1,0:T(8,128)(2,1)S(1)} %convolution_convert_fusion.1), channel_id=1, replica_groups=mesh['seq'=32,'exp'=8] {'exp'}, dimensions={0} | all-to-all | bytes 245760 | tf_op jit(solution)/shard_map/all_to_all | solution.py:174
  432.9 2.2 fusion.45
  435.2 76.5 %all-gather.12.cloned.1.call-done = bf16[1,320,6144]{1,2,0:T(8,128)(2,1)} async-done(((bf16[1,320,192]{1,2,0:T(8,128)(2,1)}), bf16[1,320,6144]{1,2,0:T(8,128)(2,1)}) %all-gather.12.cloned.1.call-update) | async-done | bytes 3932176 | tf_op jit(solution)/shard_map/all_gather | solution.py:176
  511.8 4.5 fusion
  516.6 2.7 fusion.16
  519.3 89.9 %all-gather.18.cloned.1.call-done = bf16[256,128,128]{2,1,0:T(8,128)(2,1)} async-done(((bf16[8,128,128]{2,1,0:T(8,128)(2,1)}), bf16[256,128,128]{2,1,0:T(8,128)(2,1)}) %all-gather.18.cloned.1.call-update) | async-done | bytes 8388624 | tf_op jit(solution)/shard_map/all_gather | solution.py:12
  609.3 6.3 reduce_sum.98
  615.6 85.0 %all-gather.14.cloned.1.call-done = bf16[320,9216]{0,1:T(8,128)(2,1)} async-done(((bf16[320,288]{0,1:T(8,128)(2,1)}), bf16[320,9216]{0,1:T(8,128)(2,1)}) %all-gather.14.cloned.1.call-update) | async-done | bytes 5898256 | tf_op jit(solution)/shard_map/all_gather | solution.py:186
  700.6 6.8 fusion.24
  709.7 3.2 reduce.5
  714.6 4.8 all-to-all-start.1
  720.8 3.3 all-to-all-done.1
  724.1 2.3 reshape.244
  (95 shorter events, 64.8 us)
Async XLA Ops:
  7.2 504.6 %copy-start = (bf16[1,288,6144]{2,1,0:T(8,128)(2,1)S(1)}, bf16[1,288,6144]{2,1,0:T(8,128)(2,1)}, u32[]{:S(2)}) copy-start(bf16[1,288,6144]{2,1,0:T(8,128)(2,1)} %param.31) | copy-start | bytes 10616836
  7.2 113.7 %all-gather.16.cloned.1.call-start = ((), (), s32[]{:S(2)}) async-start(), calls=%async_computation.7 | async-start | bytes 8650752 | tf_op jit(solution)/shard_map/all_gather | solution.py:20
  19.9 265.3 %all-gather.10.cloned.1.call-start = ((), (), s32[]{:S(2)}) async-start(), calls=%async_computation.3 | async-start | bytes 8650752 | tf_op jit(solution)/shard_map/all_gather | solution.py:129
  65.1 2.0 copy-start.1
  121.7 2.8 copy-start.4
  121.7 3.8 copy-start.5
  129.5 163.3 %copy-start.3 = (s32[512,2]{0,1:T(2,128)S(1)}, s32[512,2]{0,1:T(2,128)}, u32[]{:S(2)}) copy-start(s32[512,2]{0,1:T(2,128)} %param.34) | copy-start | bytes 12292
  129.5 166.4 %copy-start.8 = (u32[256]{0:T(256)S(1)}, u32[256]{0:T(256)}, u32[]{:S(2)}) copy-start(u32[256]{0:T(256)} %constant.78) | copy-start | bytes 3076
  129.5 198.6 %reduce-scatter.2.cloned.1.call-start = ((), (), s32[]{:S(2)}) async-start(), calls=%async_computation.4 | async-start | bytes 1769472 | tf_op jit(solution)/shard_map/reduce_scatter | solution.py:131
  292.7 219.0 %all-gather.12.cloned.1.call-start = ((), (), s32[]{:S(2)}) async-start(), calls=%async_computation.5 | async-start | bytes 4866048 | tf_op jit(solution)/shard_map/all_gather | solution.py:176
  416.5 2.3 copy-start.2
  432.2 177.1 %all-gather.18.cloned.1.call-start = ((), (), s32[]{:S(2)}) async-start(), calls=%async_computation.8 | async-start | bytes 8650752 | tf_op jit(solution)/shard_map/all_gather | solution.py:12
  435.2 265.4 %all-gather.14.cloned.1.call-start = ((), (), s32[]{:S(2)}) async-start(), calls=%async_computation.6 | async-start | bytes 7299072 | tf_op jit(solution)/shard_map/all_gather | solution.py:186
  511.8 4.5 copy-start.6
  511.8 4.9 copy-start.7
  714.6 9.5 %all-to-all-start.1 = ((bf16[8,2,3840]{2,1,0:T(2,128)(2,1)}), bf16[8,2,3840]{2,1,0:T(2,128)(2,1)}, u32[]{:S(2)}, u32[]{:S(2)}) async-start(bf16[8,2,3840]{2,1,0:T(2,128)(2,1)} %reshape.243), calls=%async_computation.2 | async-start | bytes 245760 | tf_op jit(solution)/shard_map/all_to_all | solution.py:191
Sparse Core Ops, SparseCore 0:
  20.0 100.8 all-gather.15
  129.6 155.5 all-gather.9
  292.9 29.4 reduce-scatter.1
  432.3 79.4 all-gather.11
  514.2 95.0 all-gather.17
  611.7 88.8 all-gather.13
